TPU v7x, 32 devices: a whole 2x2x4 slice. The times are simulated.
32 devices in a mesh: seq: 8 (over z, x), head: 4 (over y, core).
Axes of the slice: x: 2, y: 2, z: 4, core: 2. Of those that a mesh axis runs over, the one named last changes fastest.
Arguments:
- queries: bfloat16 [1024, 1536], P('seq', 'head'), may hold values from -8 to 8
- cell_types: int32 [1024], P('seq'), may hold values from 0 to 127
- promoters: int32 [1024], P('seq'), may hold values from 0 to 16383, as said below
- offsets: int32 [1024], P('seq'), may hold values from -64 to 64, as said below
- cell_embed: bfloat16 [128, 1536], P(None, 'head'), may hold values from -3 to 3
- bin_keys: bfloat16 [16384, 1536], P('seq', 'head'), may hold values from -6 to 6
- bin_values: bfloat16 [16384, 1536], P('seq', 'head'), may hold values from -6 to 6
- slopes: float32 [16], P('head'), may hold values from 1.280082e-05 to 0.05
- w_out: bfloat16 [1536, 1536], P('head'), may hold values from -0.15625 to 0.15625
Outputs:
- pooled_features: bfloat16 [1024, 1536], P('seq', 'head')
Inputs may be any that keep to these rules, and one draw needn't show every extreme that they name: `promoters`: the promoter of row r lies in bins (r // 128) * 2048 to (r // 128 + 1) * 2048 - 1; in each aligned block of 128 rows, the block's first row sits at the first of those bins and its second row at the last. `offsets`: in each aligned block of 128 rows the first row has offset -64 and the second row 64.
All inputs are finite; a program needn't handle non-finite values.
Results may differ from a plain program's by a relative error of at most 0.012.
Values may be sent and summed in bfloat16 or wider, within the bound.
A program may use at most 128 MiB of HBM per device.

v0:
```python
import functools

import jax
import jax.numpy as jnp
from jax import lax
from jax.experimental import pallas as pl
from jax.experimental.pallas import tpu as pltpu
from jax.sharding import PartitionSpec as P

HEAD_DIM = 96
RADIUS = 7812
SHIFT = 64
HOPS = 4
LANES = 128
CHUNK = 256
EXTRA = 16
LOG2E = 1.4426950408889634
FAR = -1e30


def shift_by(value, by):
    peers = lax.axis_size("seq")
    pairs = [(i, i + by) for i in range(peers) if 0 <= i + by < peers]
    return lax.ppermute(value, "seq", pairs)


def identity_mask(size):
    return lax.broadcasted_iota(jnp.int32, (size, size), 0) == lax.broadcasted_iota(
        jnp.int32, (size, size), 1
    )


def as_column(row):
    size = row.shape[1]
    return jnp.sum(jnp.where(identity_mask(size), row, 0.0), axis=1, keepdims=True)


def as_row(column):
    size = column.shape[0]
    return jnp.sum(jnp.where(identity_mask(size), column, 0.0), axis=0, keepdims=True)


def tiles_of(head):
    first = head * HEAD_DIM
    start = first // LANES * LANES
    stop = -(-(first + HEAD_DIM) // LANES) * LANES
    return first, start, stop


def attend(hop, sign, pack, k_ref, v_ref, slope_ref, score_ref, out_ref, stat_ref):
    bins = k_ref.shape[0]
    rows = pack.shape[0] - EXTRA
    width = k_ref.shape[1]
    groups = width // HEAD_DIM
    corner = pack[rows:, :rows].astype(jnp.float32)
    within = as_column(corner[0:1] * 256.0 + corner[1:2])
    signf = sign.astype(jnp.float32)
    parts = {}
    for head in range(groups):
        first, start, stop = tiles_of(head)
        slope = slope_ref[head] * LOG2E
        lane = lax.broadcasted_iota(jnp.int32, (rows, stop - start), 1) + start
        query = pack[:rows, start:stop]
        query = jnp.where((lane >= first) & (lane < first + HEAD_DIM), query, jnp.zeros_like(query))
        slot = head % 2
        top = None
        if hop is None:
            ahead = signf * bins - within
        else:
            ahead = hop * bins - signf * within
        for begin in range(0, bins, CHUNK):
            raw = lax.dot_general(
                query,
                k_ref[begin : begin + CHUNK, start:stop],
                (((1,), (1,)), ((), ())),
                preferred_element_type=jnp.float32,
            )
            index = (lax.broadcasted_iota(jnp.int32, (1, CHUNK), 1) + begin).astype(jnp.float32)
            scaled = raw * (LOG2E * HEAD_DIM**-0.5)
            if hop is None:
                score = scaled - slope * jnp.abs(index + ahead)
                if 2 * bins - 1 + SHIFT > RADIUS:
                    score = jnp.where(jnp.abs(index + ahead) <= RADIUS, score, FAR)
            else:
                signed = index * signf
                score = scaled - slope * signed
                if (hop + 1) * bins - 1 + SHIFT > RADIUS:
                    score = jnp.where(signed <= RADIUS - ahead, score, FAR)
            score_ref[slot, :, begin : begin + CHUNK] = score
            for lanes in range(0, CHUNK, LANES):
                piece = score[:, lanes : lanes + LANES]
                top = piece if top is None else jnp.maximum(top, piece)
        peak = jnp.maximum(jnp.max(top, axis=1, keepdims=True), 0.1 * FAR)
        total = None
        gained = None
        for begin in range(0, bins, CHUNK):
            exps = jnp.exp2(score_ref[slot, :, begin : begin + CHUNK] - peak)
            for lanes in range(0, CHUNK, LANES):
                piece = exps[:, lanes : lanes + LANES]
                total = piece if total is None else total + piece
            term = jnp.dot(
                exps.astype(jnp.bfloat16),
                v_ref[begin : begin + CHUNK, start:stop],
                preferred_element_type=jnp.float32,
            )
            gained = term if gained is None else gained + term
        if hop is not None:
            peak = peak - slope * ahead
        stat_ref[head : head + 1, :] = as_row(peak)
        stat_ref[groups + head : groups + head + 1, :] = as_row(
            jnp.sum(total, axis=1, keepdims=True)
        )
        for tile in range(start, stop, LANES):
            parts.setdefault(tile, []).append((first, gained[:, tile - start : tile - start + LANES]))
    for tile, pieces in parts.items():
        lane = lax.broadcasted_iota(jnp.int32, (rows, LANES), 1) + tile
        value = pieces[0][1]
        for first, piece in pieces[1:]:
            value = jnp.where(lane >= first, piece, value)
        out_ref[:, tile : tile + LANES] = value.astype(jnp.bfloat16)


def attend_kernel(hops, seq_count, *refs):
    packs = refs[: 2 * hops + 1]
    k_ref, v_ref, slope_ref, out_ref, stat_ref, score_ref, pack_ref = refs[2 * hops + 1 :]
    position = lax.axis_index("seq")
    for slot in range(2 * hops + 1):
        pack_ref[slot] = packs[slot][...]

    def run(hop, shift):
        anchor = position - shift
        slot = shift + hops

        @pl.when((anchor >= 0) & (anchor < seq_count))
        def _():
            sign = shift if hop is None else jnp.where(shift > 0, 1, -1)
            attend(
                hop, sign, pack_ref.at[slot], k_ref, v_ref, slope_ref, score_ref,
                out_ref.at[slot], stat_ref.at[slot],
            )

    def near(i, _):
        run(None, i - 1)
        return 0

    lax.fori_loop(0, 3, near, 0)
    for hop in range(2, hops + 1):

        def far(i, _, hop=hop):
            run(hop, (2 * i - 1) * hop)
            return 0

        lax.fori_loop(0, 2, far, 0)


def local(queries, cell_types, promoters, offsets, cell_embed, bin_keys, bin_values, slopes, w_out):
    seq_count = lax.axis_size("seq")
    position = lax.axis_index("seq")
    bins = bin_keys.shape[0]
    rows, width = queries.shape
    groups = slopes.shape[0]
    hops = min(HOPS, seq_count - 1)
    one_hot = (
        cell_types[:, None] == jnp.arange(cell_embed.shape[0], dtype=jnp.int32)[None, :]
    ).astype(jnp.bfloat16)
    embedded = jnp.dot(one_hot, cell_embed, preferred_element_type=jnp.float32)
    query_rows = (queries.astype(jnp.float32) + embedded).astype(jnp.bfloat16)
    within = promoters + offsets - position * bins
    high = jnp.floor_divide(within, 256)
    corner = jnp.stack([high, within - 256 * high]).astype(jnp.bfloat16)
    pack = jnp.concatenate(
        [query_rows, jnp.pad(corner, ((0, EXTRA - 2), (0, width - rows)))], axis=0
    )
    packs = [pack if d == 0 else shift_by(pack, d) for d in range(-hops, hops + 1)]
    slots = 2 * hops + 1
    vmem = pl.BlockSpec(memory_space=pltpu.VMEM)
    outs, stats = pl.pallas_call(
        functools.partial(attend_kernel, hops, seq_count),
        out_shape=(
            jax.ShapeDtypeStruct((slots, rows, width), jnp.bfloat16),
            jax.ShapeDtypeStruct((slots, 2 * groups, rows), jnp.float32),
        ),
        in_specs=[vmem] * (slots + 2) + [pl.BlockSpec(memory_space=pltpu.SMEM)],
        out_specs=(vmem, vmem),
        scratch_shapes=[
            pltpu.VMEM((2, rows, bins), jnp.float32),
            pltpu.VMEM((slots, rows + EXTRA, width), jnp.bfloat16),
        ],
    )(*packs, bin_keys, bin_values, slopes)
    peaks, totals, sums = [], [], []
    for d in range(-hops, hops + 1):
        back_out = outs[d + hops] if d == 0 else shift_by(outs[d + hops], -d)
        back_stat = stats[d + hops] if d == 0 else shift_by(stats[d + hops], -d)
        there = (position + d >= 0) & (position + d < seq_count)
        peaks.append(jnp.where(there, back_stat[:groups], FAR))
        totals.append(jnp.where(there, back_stat[groups:], 0.0))
        sums.append(jnp.where(there, back_out, 0))
    peak = functools.reduce(jnp.maximum, peaks)
    total, pooled = 0.0, 0.0
    for p, t, s in zip(peaks, totals, sums):
        factor = jnp.exp2(p - peak)
        total = total + factor * t
        pooled = pooled + s.astype(jnp.float32).reshape(rows, groups, HEAD_DIM) * factor.T[:, :, None]
    pooled = (pooled / total.T[:, :, None]).reshape(rows, width).astype(jnp.bfloat16)
    partial_sums = jnp.dot(pooled, w_out, preferred_element_type=jnp.float32)
    return lax.psum_scatter(
        partial_sums.astype(jnp.bfloat16), "head", scatter_dimension=1, tiled=True
    )


def solution(mesh):
    return jax.shard_map(
        local,
        mesh=mesh,
        in_specs=(
            P("seq", "head"),
            P("seq"),
            P("seq"),
            P("seq"),
            P(None, "head"),
            P("seq", "head"),
            P("seq", "head"),
            P("head"),
            P("head", None),
        ),
        out_specs=P("seq", "head"),
        check_vma=False,
    )
```

profile of v0, /device:TPU:3, one launch (start us, length us, event | category | flops | bytes accessed | tf_op | source)
XLA Modules:
  0.0 150.5 jit_solution(14685248700411977033)
XLA Ops:
  8.0 1.2 fusion
  9.2 4.2 %collective-permute-start.7 = (bf16[144,384]{1,0:T(8,128)(2,1)S(1)}, bf16[144,384]{1,0:T(8,128)(2,1)S(1)}, u32[]{:S(2)}, u32[]{:S(2)}) collective-permute-start(bf16[144,384]{1,0:T(8,128)(2,1)S(1)} %pad_maximum_fusion.refs_4_), channel_id=1, source_target_pairs={{0,16},{4,20},{8,24},{12,28},{1,17},{5,21},{9,25},{13,29},{2,18},{... | collective-permute-start | bytes 331784 | tf_op jit(solution)/shard_map/ppermute | solution.py:24
  13.5 1.3 collective-permute-start.6
  14.8 3.8 %collective-permute-start.5 = (bf16[144,384]{1,0:T(8,128)(2,1)S(1)}, bf16[144,384]{1,0:T(8,128)(2,1)S(1)}, u32[]{:S(2)}, u32[]{:S(2)}) collective-permute-start(bf16[144,384]{1,0:T(8,128)(2,1)S(1)} %pad_maximum_fusion.refs_4_), channel_id=1, source_target_pairs={{0,8},{4,12},{8,16},{12,20},{16,24},{20,28},{1,9},{5,13},{9,17},{1... | collective-permute-start | bytes 331784 | tf_op jit(solution)/shard_map/ppermute | solution.py:24
  18.6 2.5 %collective-permute-start.4 = (bf16[144,384]{1,0:T(8,128)(2,1)S(1)}, bf16[144,384]{1,0:T(8,128)(2,1)S(1)}, u32[]{:S(2)}, u32[]{:S(2)}) collective-permute-start(bf16[144,384]{1,0:T(8,128)(2,1)S(1)} %pad_maximum_fusion.refs_4_), channel_id=1, source_target_pairs={{0,4},{4,8},{8,12},{12,16},{16,20},{20,24},{24,28},{1,5},{5,9},{9,... | collective-permute-start | bytes 331784 | tf_op jit(solution)/shard_map/ppermute | solution.py:24
  21.1 2.8 %collective-permute-start.3 = (bf16[144,384]{1,0:T(8,128)(2,1)S(1)}, bf16[144,384]{1,0:T(8,128)(2,1)S(1)}, u32[]{:S(2)}, u32[]{:S(2)}) collective-permute-start(bf16[144,384]{1,0:T(8,128)(2,1)S(1)} %pad_maximum_fusion.refs_4_), channel_id=1, source_target_pairs={{4,0},{8,4},{12,8},{16,12},{20,16},{24,20},{28,24},{5,1},{9,5},{13... | collective-permute-start | bytes 331784 | tf_op jit(solution)/shard_map/ppermute | solution.py:24
  23.9 1.3 collective-permute-start.2
  25.2 1.3 collective-permute-start.1
  26.6 1.3 collective-permute-start
  27.9 1.8 %collective-permute-done.2.refs_2_ = bf16[144,384]{1,0:T(8,128)(2,1)S(1)} collective-permute-done((bf16[144,384]{1,0:T(8,128)(2,1)S(1)}, bf16[144,384]{1,0:T(8,128)(2,1)S(1)}, u32[]{:S(2)}, u32[]{:S(2)}) %collective-permute-start.2) | collective-permute-done | bytes 110624 | tf_op jit(solution)/shard_map/ppermute | solution.py:24
  29.7 7.3 %collective-permute-done.1.refs_1_ = bf16[144,384]{1,0:T(8,128)(2,1)S(1)} collective-permute-done((bf16[144,384]{1,0:T(8,128)(2,1)S(1)}, bf16[144,384]{1,0:T(8,128)(2,1)S(1)}, u32[]{:S(2)}, u32[]{:S(2)}) %collective-permute-start.1) | collective-permute-done | bytes 110624 | tf_op jit(solution)/shard_map/ppermute | solution.py:24
  38.3 18.1 %shard_map.91 = (bf16[9,128,384]{2,1,0:T(8,128)(2,1)}, f32[9,8,128]{2,1,0:T(8,128)}) custom-call(bf16[144,384]{1,0:T(8,128)(2,1)} %copy-done.9, bf16[144,384]{1,0:T(8,128)(2,1)} %copy-done.8, bf16[144,384]{1,0:T(8,128)(2,1)} %copy-done.7, bf16[144,384]{1,0:T(8,128)(2,1)} %copy-done.6, bf16[144,384]{1,0:T(8,128)(2,1)} %copy-done.1, ...), custom_call_target="tpu_custom_call" | custom-call | tf_op jit(solution)/shard_map/pallas_call | solution.py:177
  57.0 1.3 collective-permute-start.9
  58.3 1.3 collective-permute-start.16
  59.6 1.3 collective-permute-start.15
  60.9 1.3 collective-permute-start.14
  62.2 10.2 %collective-permute-start.13 = (f32[8,128]{1,0:T(8,128)S(1)}, f32[8,128]{1,0:T(8,128)S(1)}, u32[]{:S(2)}, u32[]{:S(2)}) collective-permute-start(f32[8,128]{1,0:T(8,128)S(1)} %get-tuple-element.25), channel_id=1, source_target_pairs={{4,0},{8,4},{12,8},{16,12},{20,16},{24,20},{28,24},{5,1},{9,5},{13... | collective-permute-start | bytes 12296 | tf_op jit(solution)/shard_map/ppermute | solution.py:24
  72.5 3.7 %collective-permute-start.12 = (f32[8,128]{1,0:T(8,128)S(1)}, f32[8,128]{1,0:T(8,128)S(1)}, u32[]{:S(2)}, u32[]{:S(2)}) collective-permute-start(f32[8,128]{1,0:T(8,128)S(1)} %get-tuple-element.26), channel_id=1, source_target_pairs={{0,4},{4,8},{8,12},{12,16},{16,20},{20,24},{24,28},{1,5},{5,9},{9,... | collective-permute-start | bytes 12296 | tf_op jit(solution)/shard_map/ppermute | solution.py:24
  76.2 4.9 %collective-permute-start.11 = (f32[8,128]{1,0:T(8,128)S(1)}, f32[8,128]{1,0:T(8,128)S(1)}, u32[]{:S(2)}, u32[]{:S(2)}) collective-permute-start(f32[8,128]{1,0:T(8,128)S(1)} %get-tuple-element.27), channel_id=1, source_target_pairs={{0,8},{4,12},{8,16},{12,20},{16,24},{20,28},{1,9},{5,13},{9,17},{1... | collective-permute-start | bytes 12296 | tf_op jit(solution)/shard_map/ppermute | solution.py:24
  81.1 4.0 %collective-permute-start.10 = (f32[8,128]{1,0:T(8,128)S(1)}, f32[8,128]{1,0:T(8,128)S(1)}, u32[]{:S(2)}, u32[]{:S(2)}) collective-permute-start(f32[8,128]{1,0:T(8,128)S(1)} %get-tuple-element.28), channel_id=1, source_target_pairs={{0,12},{4,16},{8,20},{12,24},{16,28},{1,13},{5,17},{9,21},{13,25},... | collective-permute-start | bytes 12296 | tf_op jit(solution)/shard_map/ppermute | solution.py:24
  85.1 2.0 %slice_bitcast_fusion.7 = (bf16[128,384]{1,0:T(8,128)(2,1)S(1)}, bf16[128,384]{1,0:T(8,128)(2,1)S(1)}, bf16[128,384]{1,0:T(8,128)(2,1)S(1)}, bf16[128,384]{1,0:T...) fusion(bf16[9,128,384]{2,1,0:T(8,128)(2,1)} %get-tuple-element.7), kind=kLoop, calls=%fused_computation.30 | loop fusion | bytes 1572864 | tf_op jit(solution)/shard_map/squeeze | solution.py:192
  87.1 1.3 collective-permute-start.8
  88.4 1.3 collective-permute-start.23
  89.7 1.3 collective-permute-start.22
  91.0 1.3 collective-permute-start.21
  92.3 2.8 %collective-permute-start.20 = (bf16[128,384]{1,0:T(8,128)(2,1)}, bf16[128,384]{1,0:T(8,128)(2,1)}, u32[]{:S(2)}, u32[]{:S(2)}) collective-permute-start(bf16[128,384]{1,0:T(8,128)(2,1)} %get-tuple-element.17), channel_id=1, source_target_pairs={{4,0},{8,4},{12,8},{16,12},{20,16},{24,20},{28,24},{5,1},{9,5},{13... | collective-permute-start | bytes 294920 | tf_op jit(solution)/shard_map/ppermute | solution.py:24
  96.6 3.7 %collective-permute-start.19 = (bf16[128,384]{1,0:T(8,128)(2,1)}, bf16[128,384]{1,0:T(8,128)(2,1)}, u32[]{:S(2)}, u32[]{:S(2)}) collective-permute-start(bf16[128,384]{1,0:T(8,128)(2,1)} %get-tuple-element.18), channel_id=1, source_target_pairs={{0,4},{4,8},{8,12},{12,16},{16,20},{20,24},{24,28},{1,5},{5,9},{9,... | collective-permute-start | bytes 294920 | tf_op jit(solution)/shard_map/ppermute | solution.py:24
  100.3 5.5 %collective-permute-start.18 = (bf16[128,384]{1,0:T(8,128)(2,1)S(1)}, bf16[128,384]{1,0:T(8,128)(2,1)}, u32[]{:S(2)}, u32[]{:S(2)}) collective-permute-start(bf16[128,384]{1,0:T(8,128)(2,1)S(1)} %get-tuple-element.19), channel_id=1, source_target_pairs={{0,8},{4,12},{8,16},{12,20},{16,24},{20,28},{1,9},{5,13},{9,17},{1... | collective-permute-start | bytes 294920 | tf_op jit(solution)/shard_map/ppermute | solution.py:24
  105.9 5.2 %collective-permute-start.17 = (bf16[128,384]{1,0:T(8,128)(2,1)S(1)}, bf16[128,384]{1,0:T(8,128)(2,1)}, u32[]{:S(2)}, u32[]{:S(2)}) collective-permute-start(bf16[128,384]{1,0:T(8,128)(2,1)S(1)} %get-tuple-element.20), channel_id=1, source_target_pairs={{0,12},{4,16},{8,20},{12,24},{16,28},{1,13},{5,17},{9,21},{13,25},... | collective-permute-start | bytes 294920 | tf_op jit(solution)/shard_map/ppermute | solution.py:24
  113.5 1.7 %convolution_convert_fusion = bf16[128,1536]{1,0:T(8,128)(2,1)S(1)} fusion(bf16[384,1536]{1,0:T(8,128)(2,1)S(1)} %copy-done, f32[128,384]{1,0:T(8,128)S(1)} %copy.39, f32[128,384]{1,0:T(8,128)S(1)} %copy.38, f32[128,384]{1,0:T(8,128)S(1)} %copy.37, f32[128,384]{1,0:T(8,128)S(1)} %copy.36, f32[128,384]{1,0:T(8,128)S(1)} %copy.35, f32[128,384]{1,0:T(8,128)S(1)} %copy.34, ...), kind=kOutput, calls=%fused_computation | convolution fusion | flops 153010176 | bytes 4423689 | tf_op jit(solution)/shard_map/dot_general | solution.py:205
  116.1 25.9 %reduce-scatter.4.cloned.1.call-done = bf16[384,128]{1,0:T(8,128)(2,1)} async-done(((bf16[1536,128]{1,0:T(8,128)(2,1)}), bf16[384,128]{1,0:T(8,128)(2,1)}) %reduce-scatter.4.cloned.1.call-update) | async-done | bytes 98320
  142.0 1.6 %copy.41 = bf16[128,384]{1,0:T(8,128)(2,1)} copy(bf16[128,384]{0,1:T(8,128)(2,1)} %bitcast.121) | data formatting | bytes 196608
  (77 shorter events, 8.1 us)
Async XLA Ops:
  6.5 106.9 %copy-start = (bf16[384,1536]{1,0:T(8,128)(2,1)S(1)}, bf16[384,1536]{1,0:T(8,128)(2,1)}, u32[]{:S(2)}) copy-start(bf16[384,1536]{1,0:T(8,128)(2,1)} %param.17) | copy-start | bytes 3538948
  6.5 135.5 %reduce-scatter.4.cloned.1.call-start = ((), (), s32[]{:S(2)}) async-start(), calls=%async_computation.1 | async-start | bytes 491520
  9.2 27.8 %copy-start.1 = (bf16[144,384]{1,0:T(8,128)(2,1)}, bf16[144,384]{1,0:T(8,128)(2,1)S(1)}, u32[]{:S(2)}) copy-start(bf16[144,384]{1,0:T(8,128)(2,1)S(1)} %pad_maximum_fusion.refs_4_) | copy-start | bytes 331780
  9.2 14.7 %collective-permute-start.7 = (bf16[144,384]{1,0:T(8,128)(2,1)S(1)}, bf16[144,384]{1,0:T(8,128)(2,1)S(1)}, u32[]{:S(2)}, u32[]{:S(2)}) collective-permute-start(bf16[144,384]{1,0:T(8,128)(2,1)S(1)} %pad_maximum_fusion.refs_4_), channel_id=1, source_target_pairs={{0,16},{4,20},{8,24},{12,28},{1,17},{5,21},{9,25},{13,29},{2,18},{... | collective-permute-start | bytes 331784 | tf_op jit(solution)/shard_map/ppermute | solution.py:24
  13.5 11.8 %collective-permute-start.6 = (bf16[144,384]{1,0:T(8,128)(2,1)S(1)}, bf16[144,384]{1,0:T(8,128)(2,1)S(1)}, u32[]{:S(2)}, u32[]{:S(2)}) collective-permute-start(bf16[144,384]{1,0:T(8,128)(2,1)S(1)} %pad_maximum_fusion.refs_4_), channel_id=1, source_target_pairs={{0,12},{4,16},{8,20},{12,24},{16,28},{1,13},{5,17},{9,21},{13,25},... | collective-permute-start | bytes 331784 | tf_op jit(solution)/shard_map/ppermute | solution.py:24
  14.8 11.8 %collective-permute-start.5 = (bf16[144,384]{1,0:T(8,128)(2,1)S(1)}, bf16[144,384]{1,0:T(8,128)(2,1)S(1)}, u32[]{:S(2)}, u32[]{:S(2)}) collective-permute-start(bf16[144,384]{1,0:T(8,128)(2,1)S(1)} %pad_maximum_fusion.refs_4_), channel_id=1, source_target_pairs={{0,8},{4,12},{8,16},{12,20},{16,24},{20,28},{1,9},{5,13},{9,17},{1... | collective-permute-start | bytes 331784 | tf_op jit(solution)/shard_map/ppermute | solution.py:24
  18.6 9.3 %collective-permute-start.4 = (bf16[144,384]{1,0:T(8,128)(2,1)S(1)}, bf16[144,384]{1,0:T(8,128)(2,1)S(1)}, u32[]{:S(2)}, u32[]{:S(2)}) collective-permute-start(bf16[144,384]{1,0:T(8,128)(2,1)S(1)} %pad_maximum_fusion.refs_4_), channel_id=1, source_target_pairs={{0,4},{4,8},{8,12},{12,16},{16,20},{20,24},{24,28},{1,5},{5,9},{9,... | collective-permute-start | bytes 331784 | tf_op jit(solution)/shard_map/ppermute | solution.py:24
  21.1 6.8 %collective-permute-start.3 = (bf16[144,384]{1,0:T(8,128)(2,1)S(1)}, bf16[144,384]{1,0:T(8,128)(2,1)S(1)}, u32[]{:S(2)}, u32[]{:S(2)}) collective-permute-start(bf16[144,384]{1,0:T(8,128)(2,1)S(1)} %pad_maximum_fusion.refs_4_), channel_id=1, source_target_pairs={{4,0},{8,4},{12,8},{16,12},{20,16},{24,20},{28,24},{5,1},{9,5},{13... | collective-permute-start | bytes 331784 | tf_op jit(solution)/shard_map/ppermute | solution.py:24
  23.9 13.1 %copy-start.2 = (bf16[144,384]{1,0:T(8,128)(2,1)}, bf16[144,384]{1,0:T(8,128)(2,1)S(1)}, u32[]{:S(2)}) copy-start(bf16[144,384]{1,0:T(8,128)(2,1)S(1)} %collective-permute-done.7.refs_8_) | copy-start | bytes 331780
  23.9 5.8 %collective-permute-start.2 = (bf16[144,384]{1,0:T(8,128)(2,1)S(1)}, bf16[144,384]{1,0:T(8,128)(2,1)S(1)}, u32[]{:S(2)}, u32[]{:S(2)}) collective-permute-start(bf16[144,384]{1,0:T(8,128)(2,1)S(1)} %pad_maximum_fusion.refs_4_), channel_id=1, source_target_pairs={{8,0},{12,4},{16,8},{20,12},{24,16},{28,20},{9,1},{13,5},{17,9},{2... | collective-permute-start | bytes 331784 | tf_op jit(solution)/shard_map/ppermute | solution.py:24
  25.2 11.8 %copy-start.3 = (bf16[144,384]{1,0:T(8,128)(2,1)}, bf16[144,384]{1,0:T(8,128)(2,1)S(1)}, u32[]{:S(2)}) copy-start(bf16[144,384]{1,0:T(8,128)(2,1)S(1)} %collective-permute-done.6.refs_7_) | copy-start | bytes 331780
  25.2 11.7 %collective-permute-start.1 = (bf16[144,384]{1,0:T(8,128)(2,1)S(1)}, bf16[144,384]{1,0:T(8,128)(2,1)S(1)}, u32[]{:S(2)}, u32[]{:S(2)}) collective-permute-start(bf16[144,384]{1,0:T(8,128)(2,1)S(1)} %pad_maximum_fusion.refs_4_), channel_id=1, source_target_pairs={{12,0},{16,4},{20,8},{24,12},{28,16},{13,1},{17,5},{21,9},{25,13},... | collective-permute-start | bytes 331784 | tf_op jit(solution)/shard_map/ppermute | solution.py:24
  26.6 10.5 %copy-start.4 = (bf16[144,384]{1,0:T(8,128)(2,1)}, bf16[144,384]{1,0:T(8,128)(2,1)S(1)}, u32[]{:S(2)}) copy-start(bf16[144,384]{1,0:T(8,128)(2,1)S(1)} %collective-permute-done.5.refs_6_) | copy-start | bytes 331780
  26.6 10.4 %collective-permute-start = (bf16[144,384]{1,0:T(8,128)(2,1)S(1)}, bf16[144,384]{1,0:T(8,128)(2,1)S(1)}, u32[]{:S(2)}, u32[]{:S(2)}) collective-permute-start(bf16[144,384]{1,0:T(8,128)(2,1)S(1)} %pad_maximum_fusion.refs_4_), channel_id=1, source_target_pairs={{16,0},{20,4},{24,8},{28,12},{17,1},{21,5},{25,9},{29,13},{18,2},{... | collective-permute-start | bytes 331784 | tf_op jit(solution)/shard_map/ppermute | solution.py:24
  57.0 15.4 %collective-permute-start.9 = (f32[8,128]{1,0:T(8,128)S(1)}, f32[8,128]{1,0:T(8,128)S(1)}, u32[]{:S(2)}, u32[]{:S(2)}) collective-permute-start(f32[8,128]{1,0:T(8,128)S(1)} %get-tuple-element.21), channel_id=1, source_target_pairs={{0,16},{4,20},{8,24},{12,28},{1,17},{5,21},{9,25},{13,29},{2,18},{... | collective-permute-start | bytes 12296 | tf_op jit(solution)/shard_map/ppermute | solution.py:24
  58.3 17.9 %collective-permute-start.16 = (f32[8,128]{1,0:T(8,128)S(1)}, f32[8,128]{1,0:T(8,128)S(1)}, u32[]{:S(2)}, u32[]{:S(2)}) collective-permute-start(f32[8,128]{1,0:T(8,128)S(1)} %get-tuple-element.22), channel_id=1, source_target_pairs={{16,0},{20,4},{24,8},{28,12},{17,1},{21,5},{25,9},{29,13},{18,2},{... | collective-permute-start | bytes 12296 | tf_op jit(solution)/shard_map/ppermute | solution.py:24
  59.6 21.5 %collective-permute-start.15 = (f32[8,128]{1,0:T(8,128)S(1)}, f32[8,128]{1,0:T(8,128)S(1)}, u32[]{:S(2)}, u32[]{:S(2)}) collective-permute-start(f32[8,128]{1,0:T(8,128)S(1)} %get-tuple-element.23), channel_id=1, source_target_pairs={{12,0},{16,4},{20,8},{24,12},{28,16},{13,1},{17,5},{21,9},{25,13},... | collective-permute-start | bytes 12296 | tf_op jit(solution)/shard_map/ppermute | solution.py:24
  60.9 26.1 %collective-permute-start.14 = (f32[8,128]{1,0:T(8,128)S(1)}, f32[8,128]{1,0:T(8,128)S(1)}, u32[]{:S(2)}, u32[]{:S(2)}) collective-permute-start(f32[8,128]{1,0:T(8,128)S(1)} %get-tuple-element.24), channel_id=1, source_target_pairs={{8,0},{12,4},{16,8},{20,12},{24,16},{28,20},{9,1},{13,5},{17,9},{2... | collective-permute-start | bytes 12296 | tf_op jit(solution)/shard_map/ppermute | solution.py:24
  62.2 26.1 %collective-permute-start.13 = (f32[8,128]{1,0:T(8,128)S(1)}, f32[8,128]{1,0:T(8,128)S(1)}, u32[]{:S(2)}, u32[]{:S(2)}) collective-permute-start(f32[8,128]{1,0:T(8,128)S(1)} %get-tuple-element.25), channel_id=1, source_target_pairs={{4,0},{8,4},{12,8},{16,12},{20,16},{24,20},{28,24},{5,1},{9,5},{13... | collective-permute-start | bytes 12296 | tf_op jit(solution)/shard_map/ppermute | solution.py:24
  72.5 17.2 %collective-permute-start.12 = (f32[8,128]{1,0:T(8,128)S(1)}, f32[8,128]{1,0:T(8,128)S(1)}, u32[]{:S(2)}, u32[]{:S(2)}) collective-permute-start(f32[8,128]{1,0:T(8,128)S(1)} %get-tuple-element.26), channel_id=1, source_target_pairs={{0,4},{4,8},{8,12},{12,16},{16,20},{20,24},{24,28},{1,5},{5,9},{9,... | collective-permute-start | bytes 12296 | tf_op jit(solution)/shard_map/ppermute | solution.py:24
  76.2 14.8 %collective-permute-start.11 = (f32[8,128]{1,0:T(8,128)S(1)}, f32[8,128]{1,0:T(8,128)S(1)}, u32[]{:S(2)}, u32[]{:S(2)}) collective-permute-start(f32[8,128]{1,0:T(8,128)S(1)} %get-tuple-element.27), channel_id=1, source_target_pairs={{0,8},{4,12},{8,16},{12,20},{16,24},{20,28},{1,9},{5,13},{9,17},{1... | collective-permute-start | bytes 12296 | tf_op jit(solution)/shard_map/ppermute | solution.py:24
  81.1 11.2 %collective-permute-start.10 = (f32[8,128]{1,0:T(8,128)S(1)}, f32[8,128]{1,0:T(8,128)S(1)}, u32[]{:S(2)}, u32[]{:S(2)}) collective-permute-start(f32[8,128]{1,0:T(8,128)S(1)} %get-tuple-element.28), channel_id=1, source_target_pairs={{0,12},{4,16},{8,20},{12,24},{16,28},{1,13},{5,17},{9,21},{13,25},... | collective-permute-start | bytes 12296 | tf_op jit(solution)/shard_map/ppermute | solution.py:24
  87.1 9.5 %collective-permute-start.8 = (bf16[128,384]{1,0:T(8,128)(2,1)S(1)}, bf16[128,384]{1,0:T(8,128)(2,1)S(1)}, u32[]{:S(2)}, u32[]{:S(2)}) collective-permute-start(bf16[128,384]{1,0:T(8,128)(2,1)S(1)} %get-tuple-element.13), channel_id=1, source_target_pairs={{0,16},{4,20},{8,24},{12,28},{1,17},{5,21},{9,25},{13,29},{2,18},{... | collective-permute-start | bytes 294920 | tf_op jit(solution)/shard_map/ppermute | solution.py:24
  88.4 11.9 %collective-permute-start.23 = (bf16[128,384]{1,0:T(8,128)(2,1)S(1)}, bf16[128,384]{1,0:T(8,128)(2,1)S(1)}, u32[]{:S(2)}, u32[]{:S(2)}) collective-permute-start(bf16[128,384]{1,0:T(8,128)(2,1)S(1)} %get-tuple-element.14), channel_id=1, source_target_pairs={{16,0},{20,4},{24,8},{28,12},{17,1},{21,5},{25,9},{29,13},{18,2},{... | collective-permute-start | bytes 294920 | tf_op jit(solution)/shard_map/ppermute | solution.py:24
  89.7 16.2 %collective-permute-start.22 = (bf16[128,384]{1,0:T(8,128)(2,1)S(1)}, bf16[128,384]{1,0:T(8,128)(2,1)}, u32[]{:S(2)}, u32[]{:S(2)}) collective-permute-start(bf16[128,384]{1,0:T(8,128)(2,1)S(1)} %get-tuple-element.15), channel_id=1, source_target_pairs={{12,0},{16,4},{20,8},{24,12},{28,16},{13,1},{17,5},{21,9},{25,13},... | collective-permute-start | bytes 294920 | tf_op jit(solution)/shard_map/ppermute | solution.py:24
  91.0 22.4 %collective-permute-start.21 = (bf16[128,384]{1,0:T(8,128)(2,1)}, bf16[128,384]{1,0:T(8,128)(2,1)}, u32[]{:S(2)}, u32[]{:S(2)}) collective-permute-start(bf16[128,384]{1,0:T(8,128)(2,1)} %get-tuple-element.16), channel_id=1, source_target_pairs={{8,0},{12,4},{16,8},{20,12},{24,16},{28,20},{9,1},{13,5},{17,9},{2... | collective-permute-start | bytes 294920 | tf_op jit(solution)/shard_map/ppermute | solution.py:24
  92.3 21.1 %collective-permute-start.20 = (bf16[128,384]{1,0:T(8,128)(2,1)}, bf16[128,384]{1,0:T(8,128)(2,1)}, u32[]{:S(2)}, u32[]{:S(2)}) collective-permute-start(bf16[128,384]{1,0:T(8,128)(2,1)} %get-tuple-element.17), channel_id=1, source_target_pairs={{4,0},{8,4},{12,8},{16,12},{20,16},{24,20},{28,24},{5,1},{9,5},{13... | collective-permute-start | bytes 294920 | tf_op jit(solution)/shard_map/ppermute | solution.py:24
  96.6 15.3 %copy-start.10 = (bf16[128,384]{1,0:T(8,128)(2,1)}, bf16[128,384]{1,0:T(8,128)(2,1)S(1)}, u32[]{:S(2)}) copy-start(bf16[128,384]{1,0:T(8,128)(2,1)S(1)} %collective-permute-done.8) | copy-start | bytes 294916
  96.6 16.9 %collective-permute-start.19 = (bf16[128,384]{1,0:T(8,128)(2,1)}, bf16[128,384]{1,0:T(8,128)(2,1)}, u32[]{:S(2)}, u32[]{:S(2)}) collective-permute-start(bf16[128,384]{1,0:T(8,128)(2,1)} %get-tuple-element.18), channel_id=1, source_target_pairs={{0,4},{4,8},{8,12},{12,16},{16,20},{20,24},{24,28},{1,5},{5,9},{9,... | collective-permute-start | bytes 294920 | tf_op jit(solution)/shard_map/ppermute | solution.py:24
  100.3 11.6 %copy-start.11 = (bf16[128,384]{1,0:T(8,128)(2,1)}, bf16[128,384]{1,0:T(8,128)(2,1)S(1)}, u32[]{:S(2)}) copy-start(bf16[128,384]{1,0:T(8,128)(2,1)S(1)} %collective-permute-done.23) | copy-start | bytes 294916
  100.3 13.1 %collective-permute-start.18 = (bf16[128,384]{1,0:T(8,128)(2,1)S(1)}, bf16[128,384]{1,0:T(8,128)(2,1)}, u32[]{:S(2)}, u32[]{:S(2)}) collective-permute-start(bf16[128,384]{1,0:T(8,128)(2,1)S(1)} %get-tuple-element.19), channel_id=1, source_target_pairs={{0,8},{4,12},{8,16},{12,20},{16,24},{20,28},{1,9},{5,13},{9,17},{1... | collective-permute-start | bytes 294920 | tf_op jit(solution)/shard_map/ppermute | solution.py:24
  105.9 7.6 %collective-permute-start.17 = (bf16[128,384]{1,0:T(8,128)(2,1)S(1)}, bf16[128,384]{1,0:T(8,128)(2,1)}, u32[]{:S(2)}, u32[]{:S(2)}) collective-permute-start(bf16[128,384]{1,0:T(8,128)(2,1)S(1)} %get-tuple-element.20), channel_id=1, source_target_pairs={{0,12},{4,16},{8,20},{12,24},{16,28},{1,13},{5,17},{9,21},{13,25},... | collective-permute-start | bytes 294920 | tf_op jit(solution)/shard_map/ppermute | solution.py:24
  (5 other events, 26.9 us)
Sparse Core Ops, SparseCore 0:
  116.3 25.7 reduce-scatter.3
where the time goes:
time: 153 us; the launch traced here: 150 us
  starting transfers between devices  68.9 us (45%)
  waiting for transfers between devices  35 us (23%)
  Pallas kernels  18.1 us (12%)
  between operations  14 us (9%)
  local copies, waits for them, and re-layouts  7.93 us (5%)
  other arithmetic  3.68 us (2%)
  matrix products  2.89 us (2%)
    ppermute x24, starting transfers between devices, shift_by(): return lax.ppermute(value, 'seq', pairs)  68.9 us
    unnamed x2, waiting for transfers between devices  25.9 us
    pallas_call x1, Pallas kernels, local(): pl.pallas_call(functools.partial(attend_kernel, hops, seq_count), out_sha...  18.1 us
    ppermute x24, waiting for transfers between devices, shift_by(): return lax.ppermute(value, 'seq', pairs)  9.12 us
    unnamed x26, local copies, waits for them, and re-layouts  3.81 us
  transfers between devices with their start and end apart: 25, of which 3 were waited for; matrix products, arithmetic and copies ran while one was open for 4% of the time, Pallas kernels for 0%

commit v1 on v0

--- a/solution.py
+++ b/solution.py
@@ -18,10 +18,7 @@
 FAR = -1e30
 
 
-def shift_by(value, by):
-    peers = lax.axis_size("seq")
-    pairs = [(i, i + by) for i in range(peers) if 0 <= i + by < peers]
-    return lax.ppermute(value, "seq", pairs)
+MESH = pl.DeviceIdType.MESH
 
 
 def identity_mask(size):
@@ -120,37 +117,184 @@
         out_ref[:, tile : tile + LANES] = value.astype(jnp.bfloat16)
 
 
-def attend_kernel(hops, seq_count, *refs):
-    packs = refs[: 2 * hops + 1]
-    k_ref, v_ref, slope_ref, out_ref, stat_ref, score_ref, pack_ref = refs[2 * hops + 1 :]
+def attend_kernel(
+    hops, seq_count, head_count,
+    pack_in, k_hbm, v_hbm, w_hbm, slope_ref, result_ref,
+    k_ref, v_ref, w_ref, pack_ref, out_ref, stat_ref, back_ref, back_stat_ref,
+    score_ref, sum_ref, part_ref, head_ref,
+    load_sem, q_send, q_recv, o_send, o_recv, s_send, s_recv, h_send, h_recv,
+):
     position = lax.axis_index("seq")
-    for slot in range(2 * hops + 1):
-        pack_ref[slot] = packs[slot][...]
+    mine = lax.axis_index("head")
+    rows, width = out_ref.shape[1:]
+    groups = width // HEAD_DIM
+    piece = result_ref.shape[1]
+    loads = [
+        pltpu.make_async_copy(src, dst, load_sem.at[i])
+        for i, (src, dst) in enumerate(((k_hbm, k_ref), (v_hbm, v_ref), (w_hbm, w_ref)))
+    ]
+    for load in loads:
+        load.start()
+
+    def inside(index):
+        return (index >= 0) & (index < seq_count)
+
+    barrier = pltpu.get_barrier_semaphore()
+    offsets = [sign * hop for hop in range(1, hops + 1) for sign in (1, -1)]
+    for d in offsets:
+
+        @pl.when(inside(position + d))
+        def _(d=d):
+            pl.semaphore_signal(
+                barrier, inc=1, device_id=(position + d, mine), device_id_type=MESH
+            )
+
+    for r in range(1, head_count):
+        pl.semaphore_signal(
+            barrier, inc=1, device_id=(position, lax.rem(mine + r, head_count)), device_id_type=MESH
+        )
+    around = jnp.minimum(position, hops) + jnp.minimum(seq_count - 1 - position, hops)
+    pl.semaphore_wait(barrier, around + head_count - 1)
+
+    def query_copy(slot, target):
+        return pltpu.make_async_remote_copy(
+            src_ref=pack_in, dst_ref=pack_ref.at[slot], send_sem=q_send.at[slot],
+            recv_sem=q_recv.at[slot], device_id=(target, mine), device_id_type=MESH,
+        )
+
+    def out_copy(slot, target):
+        return pltpu.make_async_remote_copy(
+            src_ref=out_ref.at[slot], dst_ref=back_ref.at[slot], send_sem=o_send.at[slot],
+            recv_sem=o_recv.at[slot], device_id=(target, mine), device_id_type=MESH,
+        )
+
+    def stat_copy(slot, target):
+        return pltpu.make_async_remote_copy(
+            src_ref=stat_ref.at[slot], dst_ref=back_stat_ref.at[slot], send_sem=s_send.at[slot],
+            recv_sem=s_recv.at[slot], device_id=(target, mine), device_id_type=MESH,
+        )
+
+    order = [1] + list(range(hops, 1, -1))
+    for hop in order:
+        for d in (hop, -hop):
+
+            @pl.when(inside(position + d))
+            def _(d=d):
+                query_copy(d + hops, position + d).start()
+
+    pack_ref[hops] = pack_in[...]
+    loads[0].wait()
+    loads[1].wait()
 
     def run(hop, shift):
         anchor = position - shift
         slot = shift + hops
 
-        @pl.when((anchor >= 0) & (anchor < seq_count))
+        @pl.when(inside(anchor))
         def _():
             sign = shift if hop is None else jnp.where(shift > 0, 1, -1)
+
+            @pl.when(shift != 0)
+            def _():
+                query_copy(slot, anchor).wait_recv()
+
             attend(
                 hop, sign, pack_ref.at[slot], k_ref, v_ref, slope_ref, score_ref,
                 out_ref.at[slot], stat_ref.at[slot],
             )
 
+            @pl.when(shift != 0)
+            def _():
+                stat_copy(slot, anchor).start()
+                out_copy(slot, anchor).start()
+
     def near(i, _):
-        run(None, i - 1)
+        run(None, i - 3 * (i // 2))
         return 0
 
     lax.fori_loop(0, 3, near, 0)
-    for hop in range(2, hops + 1):
+    for hop in order[1:]:
 
         def far(i, _, hop=hop):
             run(hop, (2 * i - 1) * hop)
             return 0
 
         lax.fori_loop(0, 2, far, 0)
+
+    back_stat_ref[hops] = stat_ref[hops]
+    for d in offsets:
+        slot = d + hops
+
+        @pl.when(inside(position + d))
+        def _(d=d, slot=slot):
+            stat_copy(slot, position + d).wait_recv()
+
+        @pl.when(jnp.logical_not(inside(position + d)))
+        def _(slot=slot):
+            back_stat_ref[slot, :groups, :] = jnp.full((groups, rows), FAR, jnp.float32)
+            back_stat_ref[slot, groups:, :] = jnp.zeros((groups, rows), jnp.float32)
+
+    slots = 2 * hops + 1
+    peak = back_stat_ref[0, :groups, :]
+    for slot in range(1, slots):
+        peak = jnp.maximum(peak, back_stat_ref[slot, :groups, :])
+    factors = [jnp.exp2(back_stat_ref[slot, :groups, :] - peak) for slot in range(slots)]
+    total = factors[0] * back_stat_ref[0, groups:, :]
+    for slot in range(1, slots):
+        total = total + factors[slot] * back_stat_ref[slot, groups:, :]
+    lane = lax.broadcasted_iota(jnp.int32, (rows, width), 1)
+
+    def spread(factor):
+        columns = factor.T
+        wide = columns[:, 0:1]
+        for head in range(1, groups):
+            wide = jnp.where(lane >= head * HEAD_DIM, columns[:, head : head + 1], wide)
+        return wide
+
+    sum_ref[...] = out_ref[hops].astype(jnp.float32) * spread(factors[hops] / total)
+    for d in offsets:
+        slot = d + hops
+
+        @pl.when(inside(position + d))
+        def _(d=d, slot=slot):
+            out_copy(slot, position + d).wait_recv()
+            sum_ref[...] += back_ref[slot].astype(jnp.float32) * spread(factors[slot] / total)
+
+    pooled = sum_ref[...].astype(jnp.bfloat16)
+    loads[2].wait()
+
+    def head_copy(r, target):
+        return pltpu.make_async_remote_copy(
+            src_ref=part_ref.at[r - 1], dst_ref=head_ref.at[r - 1], send_sem=h_send.at[r - 1],
+            recv_sem=h_recv.at[r - 1], device_id=(position, target), device_id_type=MESH,
+        )
+
+    def share(target):
+        columns = pl.ds(pl.multiple_of(target * piece, piece), piece)
+        return jnp.dot(pooled, w_ref[:, columns], preferred_element_type=jnp.float32)
+
+    for r in range(1, head_count):
+        target = lax.rem(mine + r, head_count)
+        part_ref[r - 1] = share(target).astype(jnp.bfloat16)
+        head_copy(r, target).start()
+    result = share(mine)
+    for r in range(1, head_count):
+        head_copy(r, lax.rem(mine + r, head_count)).wait_recv()
+        result = result + head_ref[r - 1].astype(jnp.float32)
+    result_ref[...] = result.astype(jnp.bfloat16)
+
+    for r in range(1, head_count):
+        head_copy(r, lax.rem(mine + r, head_count)).wait_send()
+    for d in offsets:
+
+        @pl.when(inside(position + d))
+        def _(d=d):
+            query_copy(d + hops, position + d).wait_send()
+
+        @pl.when(inside(position - d))
+        def _(d=d):
+            stat_copy(d + hops, position - d).wait_send()
+            out_copy(d + hops, position - d).wait_send()
 
 
 def local(queries, cell_types, promoters, offsets, cell_embed, bin_keys, bin_values, slopes, w_out):
@@ -171,41 +315,35 @@
     pack = jnp.concatenate(
         [query_rows, jnp.pad(corner, ((0, EXTRA - 2), (0, width - rows)))], axis=0
     )
-    packs = [pack if d == 0 else shift_by(pack, d) for d in range(-hops, hops + 1)]
+    head_count = lax.axis_size("head")
     slots = 2 * hops + 1
+    piece = w_out.shape[1] // head_count
     vmem = pl.BlockSpec(memory_space=pltpu.VMEM)
-    outs, stats = pl.pallas_call(
-        functools.partial(attend_kernel, hops, seq_count),
-        out_shape=(
-            jax.ShapeDtypeStruct((slots, rows, width), jnp.bfloat16),
-            jax.ShapeDtypeStruct((slots, 2 * groups, rows), jnp.float32),
-        ),
-        in_specs=[vmem] * (slots + 2) + [pl.BlockSpec(memory_space=pltpu.SMEM)],
-        out_specs=(vmem, vmem),
+    anywhere = pl.BlockSpec(memory_space=pl.ANY)
+    return pl.pallas_call(
+        functools.partial(attend_kernel, hops, seq_count, head_count),
+        out_shape=jax.ShapeDtypeStruct((rows, piece), jnp.bfloat16),
+        in_specs=[vmem] + [anywhere] * 3 + [pl.BlockSpec(memory_space=pltpu.SMEM)],
+        out_specs=vmem,
         scratch_shapes=[
+            pltpu.VMEM((bins, width), jnp.bfloat16),
+            pltpu.VMEM((bins, width), jnp.bfloat16),
+            pltpu.VMEM(w_out.shape, jnp.bfloat16),
+            pltpu.VMEM((slots, rows + EXTRA, width), jnp.bfloat16),
+            pltpu.VMEM((slots, rows, width), jnp.bfloat16),
+            pltpu.VMEM((slots, 2 * groups, rows), jnp.float32),
+            pltpu.VMEM((slots, rows, width), jnp.bfloat16),
+            pltpu.VMEM((slots, 2 * groups, rows), jnp.float32),
             pltpu.VMEM((2, rows, bins), jnp.float32),
-            pltpu.VMEM((slots, rows + EXTRA, width), jnp.bfloat16),
-        ],
-    )(*packs, bin_keys, bin_values, slopes)
-    peaks, totals, sums = [], [], []
-    for d in range(-hops, hops + 1):
-        back_out = outs[d + hops] if d == 0 else shift_by(outs[d + hops], -d)
-        back_stat = stats[d + hops] if d == 0 else shift_by(stats[d + hops], -d)
-        there = (position + d >= 0) & (position + d < seq_count)
-        peaks.append(jnp.where(there, back_stat[:groups], FAR))
-        totals.append(jnp.where(there, back_stat[groups:], 0.0))
-        sums.append(jnp.where(there, back_out, 0))
-    peak = functools.reduce(jnp.maximum, peaks)
-    total, pooled = 0.0, 0.0
-    for p, t, s in zip(peaks, totals, sums):
-        factor = jnp.exp2(p - peak)
-        total = total + factor * t
-        pooled = pooled + s.astype(jnp.float32).reshape(rows, groups, HEAD_DIM) * factor.T[:, :, None]
-    pooled = (pooled / total.T[:, :, None]).reshape(rows, width).astype(jnp.bfloat16)
-    partial_sums = jnp.dot(pooled, w_out, preferred_element_type=jnp.float32)
-    return lax.psum_scatter(
-        partial_sums.astype(jnp.bfloat16), "head", scatter_dimension=1, tiled=True
-    )
+            pltpu.VMEM((rows, width), jnp.float32),
+            pltpu.VMEM((head_count - 1, rows, piece), jnp.bfloat16),
+            pltpu.VMEM((head_count - 1, rows, piece), jnp.bfloat16),
+            pltpu.SemaphoreType.DMA((3,)),
+        ]
+        + [pltpu.SemaphoreType.DMA((slots,))] * 6
+        + [pltpu.SemaphoreType.DMA((head_count - 1,))] * 2,
+        compiler_params=pltpu.CompilerParams(collective_id=0, has_side_effects=True),
+    )(pack, bin_keys, bin_values, w_out, slopes)
 
 
 def solution(mesh):

time: 153 us -> 48.1 us (0.31); the launches traced: 150 us -> 47.9 us
  starting transfers between devices: 68.9 us -> 0 us
  waiting for transfers between devices: 35 us -> 0 us
  Pallas kernels: 18.1 us -> 43.1 us
  between operations: 14 us -> 0.02 us
  local copies, waits for them, and re-layouts: 7.93 us -> 1.55 us
  matrix products: 2.89 us -> 1.14 us
  other arithmetic: 3.68 us -> 2.06 us
    ppermute x24 -> x0, starting transfers between devices: 68.9 us -> none  [shift_by(): return lax.ppermute(value, 'seq', pairs)]
    unnamed x2 -> x0, waiting for transfers between devices: 25.9 us -> none
    pallas_call x1, Pallas kernels: 18.1 us -> 43.1 us  [local(): pl.pallas_call(functools.partial(attend_kernel, hops, seq_count, head_cou...]
    ppermute x24 -> x0, waiting for transfers between devices: 9.12 us -> none  [shift_by(): return lax.ppermute(value, 'seq', pairs)]
    squeeze x2 -> x0, local copies, waits for them, and re-layouts: 2.69 us -> none  [the longest x1 1.97 us: local(): back_out = outs[d + hops] if d == 0 else shift_by(outs[d + hops], -d)]
    unnamed x26 -> x3, local copies, waits for them, and re-layouts: 3.81 us -> 1.55 us
    transpose x3 -> x0, other arithmetic: 2.19 us -> none  [the longest x2 1.41 us: local(): factor.T[:, :, None]]
    dot_general x1 -> x0, matrix products: 1.71 us -> none  [local(): partial_sums = jnp.dot(pooled, w_out, preferred_element_type=jnp.float32)]
  transfers between devices with their start and end apart: 25 -> 0, of which waited for: 3 -> 0; matrix products, arithmetic and copies ran while one was open for 4% -> 0% of each run, Pallas kernels for 0% -> 0%
where the time goes in v1:
time: 48.1 us; the launch traced here: 47.9 us
  Pallas kernels  43.1 us (90%)
  other arithmetic  2.06 us (4%)
  local copies, waits for them, and re-layouts  1.55 us (3%)
  matrix products  1.14 us (2%)
    pallas_call x1, Pallas kernels, local(): pl.pallas_call(functools.partial(attend_kernel, hops, seq_count, head_cou...  43.1 us
    unnamed x3, local copies, waits for them, and re-layouts  1.55 us
    another operation x3, other arithmetic, local(): corner = jnp.stack([high, within - 256 * high]).astype(jnp.bfloat16)  1.41 us
    dot_general x1, matrix products, local(): embedded = jnp.dot(one_hot, cell_embed, preferred_element_type=jnp.float32)  1.14 us

profile of v1, /device:TPU:3, one launch (start us, length us, event | category | flops | bytes accessed | tf_op | source)
XLA Modules:
  0.0 47.9 jit_solution(15616502429707693297)
XLA Ops:
  0.0 0.0 copy-start
  0.0 0.7 %convert_bitcast_fusion.1 = (bf16[1,128]{1,0:T(2,128)(2,1)S(1)}, s32[128]{0:T(128)S(1)}) fusion(s32[]{:T(128)S(6)} %mul.7, s32[128]{0:T(128)} %param.11, s32[128]{0:T(128)} %param.12), kind=kLoop, calls=%fused_computation.18 | loop fusion | flops 2304 | bytes 1796 | tf_op jit(solution)/shard_map/stack | solution.py:314
  0.7 0.7 %convert_bitcast_fusion = bf16[1,128]{1,0:T(2,128)(2,1)S(1)} fusion(s32[128]{0:T(128)S(1)} %get-tuple-element.6, s32[]{:T(128)S(6)} %mul.7, s32[128]{0:T(128)} %param.11, s32[128]{0:T(128)} %param.12), kind=kLoop, calls=%fused_computation.17 | loop fusion | flops 640 | bytes 1796 | tf_op jit(solution)/shard_map/stack | solution.py:314
  1.4 0.0 copy-done
  1.4 1.1 %fusion = bf16[128,384]{1,0:T(8,128)(2,1)S(1)} fusion(bf16[128,384]{1,0:T(8,128)(2,1)S(1)} %copy-done, bf16[128,384]{1,0:T(8,128)(2,1)} %param.9, s32[128]{0:T(128)} %param.10), kind=kOutput, calls=%fused_computation.1 | convolution fusion | flops 12746752 | bytes 295424 | tf_op jit(solution)/shard_map/dot_general | solution.py:310
  2.6 0.6 %pad_maximum_fusion.pack_in = bf16[144,384]{1,0:T(8,128)(2,1)} fusion(bf16[16,384]{1,0:T(8,128)(2,1)S(1)} %fusion.7, bf16[128,384]{1,0:T(8,128)(2,1)S(1)} %fusion), kind=kLoop, calls=%fused_computation.2 | loop fusion | flops 221184 | bytes 221184 | tf_op jit(solution)/shard_map/concatenate | solution.py:315
  3.2 43.1 %shard_map.91 = bf16[128,384]{1,0:T(8,128)(2,1)} custom-call(bf16[144,384]{1,0:T(8,128)(2,1)} %pad_maximum_fusion.pack_in, bf16[2048,384]{1,0:T(8,128)(2,1)} %k_hbm.1, bf16[2048,384]{1,0:T(8,128)(2,1)} %v_hbm.1, bf16[384,1536]{1,0:T(8,128)(2,1)} %w_hbm.1, f32[4]{0:T(128)} %slope_ref.1), custom_call_target="tpu_custom_call" | custom-call | tf_op jit(solution)/shard_map/pallas_call | solution.py:323
  46.3 1.5 %copy.11 = bf16[128,384]{1,0:T(8,128)(2,1)} copy(bf16[128,384]{1,0:T(8,128)(2,1)} %shard_map.91) | data formatting | bytes 196608
  (1 shorter events, 0.0 us)
Async XLA Ops:
  0.0 1.4 %copy-start = (bf16[128,384]{1,0:T(8,128)(2,1)S(1)}, bf16[128,384]{1,0:T(8,128)(2,1)}, u32[]{:S(2)}) copy-start(bf16[128,384]{1,0:T(8,128)(2,1)} %param.13) | copy-start | bytes 294916

commit v2 on v1

--- a/solution.py
+++ b/solution.py
@@ -119,7 +119,8 @@
 
 def attend_kernel(
     hops, seq_count, head_count,
-    pack_in, k_hbm, v_hbm, w_hbm, slope_ref, result_ref,
+    query_ref, type_ref, promoter_ref, offset_ref, embed_ref, k_hbm, v_hbm, w_hbm, slope_ref,
+    result_ref,
     k_ref, v_ref, w_ref, pack_ref, out_ref, stat_ref, back_ref, back_stat_ref,
     score_ref, sum_ref, part_ref, head_ref,
     load_sem, q_send, q_recv, o_send, o_recv, s_send, s_recv, h_send, h_recv,
@@ -153,12 +154,29 @@
         pl.semaphore_signal(
             barrier, inc=1, device_id=(position, lax.rem(mine + r, head_count)), device_id_type=MESH
         )
+
+    bins = k_ref.shape[0]
+    chosen = (
+        lax.broadcasted_iota(jnp.int32, (embed_ref.shape[0], rows), 0) == type_ref[...]
+    ).astype(jnp.float32)
+    embedded = jnp.dot(
+        chosen.T.astype(jnp.bfloat16), embed_ref[...], preferred_element_type=jnp.float32
+    )
+    home = pack_ref.at[hops]
+    home[:rows, :] = (query_ref[...].astype(jnp.float32) + embedded).astype(jnp.bfloat16)
+    within = promoter_ref[...] + offset_ref[...] - position * bins
+    high = lax.shift_right_arithmetic(within, 8)
+    digit = lax.broadcasted_iota(jnp.int32, (EXTRA, rows), 0)
+    corner = jnp.where(digit == 0, high, within - 256 * high).astype(jnp.float32)
+    home[rows:, :] = jnp.zeros((EXTRA, width), jnp.bfloat16)
+    home[rows:, :rows] = corner.astype(jnp.bfloat16)
+
     around = jnp.minimum(position, hops) + jnp.minimum(seq_count - 1 - position, hops)
     pl.semaphore_wait(barrier, around + head_count - 1)
 
     def query_copy(slot, target):
         return pltpu.make_async_remote_copy(
-            src_ref=pack_in, dst_ref=pack_ref.at[slot], send_sem=q_send.at[slot],
+            src_ref=pack_ref.at[hops], dst_ref=pack_ref.at[slot], send_sem=q_send.at[slot],
             recv_sem=q_recv.at[slot], device_id=(target, mine), device_id_type=MESH,
         )
 
@@ -182,7 +200,6 @@
             def _(d=d):
                 query_copy(d + hops, position + d).start()
 
-    pack_ref[hops] = pack_in[...]
     loads[0].wait()
     loads[1].wait()
 
@@ -281,7 +298,7 @@
     for r in range(1, head_count):
         head_copy(r, lax.rem(mine + r, head_count)).wait_recv()
         result = result + head_ref[r - 1].astype(jnp.float32)
-    result_ref[...] = result.astype(jnp.bfloat16)
+    result_ref[...] = result
 
     for r in range(1, head_count):
         head_copy(r, lax.rem(mine + r, head_count)).wait_send()
@@ -299,31 +316,19 @@
 
 def local(queries, cell_types, promoters, offsets, cell_embed, bin_keys, bin_values, slopes, w_out):
     seq_count = lax.axis_size("seq")
-    position = lax.axis_index("seq")
     bins = bin_keys.shape[0]
     rows, width = queries.shape
     groups = slopes.shape[0]
     hops = min(HOPS, seq_count - 1)
-    one_hot = (
-        cell_types[:, None] == jnp.arange(cell_embed.shape[0], dtype=jnp.int32)[None, :]
-    ).astype(jnp.bfloat16)
-    embedded = jnp.dot(one_hot, cell_embed, preferred_element_type=jnp.float32)
-    query_rows = (queries.astype(jnp.float32) + embedded).astype(jnp.bfloat16)
-    within = promoters + offsets - position * bins
-    high = jnp.floor_divide(within, 256)
-    corner = jnp.stack([high, within - 256 * high]).astype(jnp.bfloat16)
-    pack = jnp.concatenate(
-        [query_rows, jnp.pad(corner, ((0, EXTRA - 2), (0, width - rows)))], axis=0
-    )
     head_count = lax.axis_size("head")
     slots = 2 * hops + 1
     piece = w_out.shape[1] // head_count
     vmem = pl.BlockSpec(memory_space=pltpu.VMEM)
     anywhere = pl.BlockSpec(memory_space=pl.ANY)
-    return pl.pallas_call(
+    result = pl.pallas_call(
         functools.partial(attend_kernel, hops, seq_count, head_count),
-        out_shape=jax.ShapeDtypeStruct((rows, piece), jnp.bfloat16),
-        in_specs=[vmem] + [anywhere] * 3 + [pl.BlockSpec(memory_space=pltpu.SMEM)],
+        out_shape=jax.ShapeDtypeStruct((rows, piece), jnp.float32),
+        in_specs=[vmem] * 5 + [anywhere] * 3 + [pl.BlockSpec(memory_space=pltpu.SMEM)],
         out_specs=vmem,
         scratch_shapes=[
             pltpu.VMEM((bins, width), jnp.bfloat16),
@@ -343,7 +348,18 @@
         + [pltpu.SemaphoreType.DMA((slots,))] * 6
         + [pltpu.SemaphoreType.DMA((head_count - 1,))] * 2,
         compiler_params=pltpu.CompilerParams(collective_id=0, has_side_effects=True),
-    )(pack, bin_keys, bin_values, w_out, slopes)
+    )(
+        queries,
+        cell_types[None],
+        promoters[None],
+        offsets[None],
+        cell_embed,
+        bin_keys,
+        bin_values,
+        w_out,
+        slopes,
+    )
+    return result.astype(jnp.bfloat16)
 
 
 def solution(mesh):

time: 48.1 us -> 45 us (0.936)
  local copies, waits for them, and re-layouts: 1.55 us -> 0 us
  matrix products: 1.14 us -> 0 us
    convert_element_type x0 -> x1, other arithmetic: none -> 1.58 us  [local(): return result.astype(jnp.bfloat16)]
    unnamed x3 -> x0, local copies, waits for them, and re-layouts: 1.55 us -> none
    another operation x3 -> x0, other arithmetic: 1.41 us -> none  [local(): corner = jnp.stack([high, within - 256 * high]).astype(jnp.bfloat16)]
    dot_general x1 -> x0, matrix products: 1.14 us -> none  [local(): embedded = jnp.dot(one_hot, cell_embed, preferred_element_type=jnp.float32)]
    concatenate x1 -> x0, other arithmetic: 0.65 us -> none  [local(): jnp.concatenate([query_rows, jnp.pad(corner, ((0, EXTRA - 2), (0, width -...]
where the time goes in v2:
time: 45 us; the launch traced here: 44.9 us
  Pallas kernels  43.3 us (96%)
  other arithmetic  1.58 us (4%)
    pallas_call x1, Pallas kernels, local(): pl.pallas_call(functools.partial(attend_kernel, hops, seq_count, head_cou...  43.3 us
    convert_element_type x1, other arithmetic, local(): return result.astype(jnp.bfloat16)  1.58 us

profile of v2, /device:TPU:3, one launch (start us, length us, event | category | flops | bytes accessed | tf_op | source)
XLA Modules:
  0.0 44.9 jit_solution(10036344779905434225)
XLA Ops:
  0.0 43.3 %shard_map.91 = f32[128,384]{1,0:T(8,128)} custom-call(bf16[128,384]{1,0:T(8,128)(2,1)} %query_ref.1, s32[1,128]{1,0:T(1,128)} %bitcast.3, s32[1,128]{1,0:T(1,128)} %bitcast.4, s32[1,128]{1,0:T(1,128)} %bitcast.5, bf16[128,384]{1,0:T(8,128)(2,1)} %embed_ref.1, bf16[2048,384]{1,0:T(8,128)(2,1)} %k_hbm.1, bf16[2048,384]{1,0:T(8,128)(2,1)} %v_hbm.1, ...), custom_call_target="tpu_custom_call" | custom-call | tf_op jit(solution)/shard_map/pallas_call | solution.py:328
  43.3 1.6 %convert_element_type.3 = bf16[128,384]{1,0:T(8,128)(2,1)} convert(f32[128,384]{1,0:T(8,128)} %shard_map.91) | non-fusion elementwise | flops 49152 | bytes 294912 | tf_op jit(solution)/shard_map/convert_element_type | solution.py:362

commit v3 on v2

--- a/solution.py
+++ b/solution.py
@@ -44,27 +44,27 @@
     return first, start, stop
 
 
-def attend(hop, sign, pack, k_ref, v_ref, slope_ref, score_ref, out_ref, stat_ref):
+def attend(hop, signs, slots, pack_ref, k_ref, v_ref, slope_ref, score_ref, out_ref, stat_ref):
     bins = k_ref.shape[0]
-    rows = pack.shape[0] - EXTRA
+    rows = pack_ref.shape[1] - EXTRA
     width = k_ref.shape[1]
     groups = width // HEAD_DIM
-    corner = pack[rows:, :rows].astype(jnp.float32)
-    within = as_column(corner[0:1] * 256.0 + corner[1:2])
-    signf = sign.astype(jnp.float32)
-    parts = {}
+    count = len(signs)
+    aheads = []
+    for sign, slot in zip(signs, slots):
+        corner = pack_ref[slot, rows:, :rows].astype(jnp.float32)
+        within = as_column(corner[0:1] * 256.0 + corner[1:2])
+        aheads.append(hop * bins - sign * within if hop >= 2 else sign * hop * bins - within)
+    parts = [{} for _ in signs]
     for head in range(groups):
         first, start, stop = tiles_of(head)
         slope = slope_ref[head] * LOG2E
-        lane = lax.broadcasted_iota(jnp.int32, (rows, stop - start), 1) + start
-        query = pack[:rows, start:stop]
+        lane = lax.broadcasted_iota(jnp.int32, (count * rows, stop - start), 1) + start
+        query = [pack_ref[slot, :rows, start:stop] for slot in slots]
+        query = jnp.concatenate(query, axis=0) if count > 1 else query[0]
         query = jnp.where((lane >= first) & (lane < first + HEAD_DIM), query, jnp.zeros_like(query))
-        slot = head % 2
-        top = None
-        if hop is None:
-            ahead = signf * bins - within
-        else:
-            ahead = hop * bins - signf * within
+        buffer = head % 2
+        tops = [None] * count
         for begin in range(0, bins, CHUNK):
             raw = lax.dot_general(
                 query,
@@ -73,48 +73,61 @@
                 preferred_element_type=jnp.float32,
             )
             index = (lax.broadcasted_iota(jnp.int32, (1, CHUNK), 1) + begin).astype(jnp.float32)
-            scaled = raw * (LOG2E * HEAD_DIM**-0.5)
-            if hop is None:
-                score = scaled - slope * jnp.abs(index + ahead)
-                if 2 * bins - 1 + SHIFT > RADIUS:
-                    score = jnp.where(jnp.abs(index + ahead) <= RADIUS, score, FAR)
-            else:
-                signed = index * signf
-                score = scaled - slope * signed
-                if (hop + 1) * bins - 1 + SHIFT > RADIUS:
-                    score = jnp.where(signed <= RADIUS - ahead, score, FAR)
-            score_ref[slot, :, begin : begin + CHUNK] = score
-            for lanes in range(0, CHUNK, LANES):
-                piece = score[:, lanes : lanes + LANES]
-                top = piece if top is None else jnp.maximum(top, piece)
-        peak = jnp.maximum(jnp.max(top, axis=1, keepdims=True), 0.1 * FAR)
-        total = None
+            for i, sign in enumerate(signs):
+                scaled = raw[i * rows : (i + 1) * rows] * (LOG2E * HEAD_DIM**-0.5)
+                if hop < 2:
+                    distance = jnp.abs(index + aheads[i])
+                    score = scaled - slope * distance
+                    if (hop + 1) * bins - 1 + SHIFT > RADIUS:
+                        score = jnp.where(distance <= RADIUS, score, FAR)
+                else:
+                    signed = index * float(sign)
+                    score = scaled - slope * signed
+                    farthest = begin + CHUNK - 1 if sign > 0 else bins - 1 - begin
+                    if hop * bins + farthest + SHIFT > RADIUS:
+                        score = jnp.where(signed <= RADIUS - aheads[i], score, FAR)
+                score_ref[buffer, i * rows : (i + 1) * rows, begin : begin + CHUNK] = score
+                for lanes in range(0, CHUNK, LANES):
+                    piece = score[:, lanes : lanes + LANES]
+                    tops[i] = piece if tops[i] is None else jnp.maximum(tops[i], piece)
+        peaks = [
+            jnp.maximum(jnp.max(top, axis=1, keepdims=True), 0.1 * FAR) for top in tops
+        ]
+        totals = [None] * count
         gained = None
         for begin in range(0, bins, CHUNK):
-            exps = jnp.exp2(score_ref[slot, :, begin : begin + CHUNK] - peak)
-            for lanes in range(0, CHUNK, LANES):
-                piece = exps[:, lanes : lanes + LANES]
-                total = piece if total is None else total + piece
+            weights = []
+            for i in range(count):
+                exps = jnp.exp2(
+                    score_ref[buffer, i * rows : (i + 1) * rows, begin : begin + CHUNK] - peaks[i]
+                )
+                for lanes in range(0, CHUNK, LANES):
+                    piece = exps[:, lanes : lanes + LANES]
+                    totals[i] = piece if totals[i] is None else totals[i] + piece
+                weights.append(exps.astype(jnp.bfloat16))
             term = jnp.dot(
-                exps.astype(jnp.bfloat16),
+                jnp.concatenate(weights, axis=0) if count > 1 else weights[0],
                 v_ref[begin : begin + CHUNK, start:stop],
                 preferred_element_type=jnp.float32,
             )
             gained = term if gained is None else gained + term
-        if hop is not None:
-            peak = peak - slope * ahead
-        stat_ref[head : head + 1, :] = as_row(peak)
-        stat_ref[groups + head : groups + head + 1, :] = as_row(
-            jnp.sum(total, axis=1, keepdims=True)
-        )
-        for tile in range(start, stop, LANES):
-            parts.setdefault(tile, []).append((first, gained[:, tile - start : tile - start + LANES]))
-    for tile, pieces in parts.items():
-        lane = lax.broadcasted_iota(jnp.int32, (rows, LANES), 1) + tile
-        value = pieces[0][1]
-        for first, piece in pieces[1:]:
-            value = jnp.where(lane >= first, piece, value)
-        out_ref[:, tile : tile + LANES] = value.astype(jnp.bfloat16)
+        for i, slot in enumerate(slots):
+            peak = peaks[i] - slope * aheads[i] if hop >= 2 else peaks[i]
+            stat_ref[slot, head : head + 1, :] = as_row(peak)
+            stat_ref[slot, groups + head : groups + head + 1, :] = as_row(
+                jnp.sum(totals[i], axis=1, keepdims=True)
+            )
+            for tile in range(start, stop, LANES):
+                parts[i].setdefault(tile, []).append(
+                    (first, gained[i * rows : (i + 1) * rows, tile - start : tile - start + LANES])
+                )
+    for i, slot in enumerate(slots):
+        for tile, pieces in parts[i].items():
+            lane = lax.broadcasted_iota(jnp.int32, (rows, LANES), 1) + tile
+            value = pieces[0][1]
+            for first, piece in pieces[1:]:
+                value = jnp.where(lane >= first, piece, value)
+            out_ref[slot, :, tile : tile + LANES] = value.astype(jnp.bfloat16)
 
 
 def attend_kernel(
@@ -200,43 +213,40 @@
             def _(d=d):
                 query_copy(d + hops, position + d).start()
 
+    for d in offsets:
+
+        @pl.when(jnp.logical_not(inside(position - d)))
+        def _(d=d):
+            pack_ref[d + hops] = jnp.zeros((rows + EXTRA, width), jnp.bfloat16)
+
     loads[0].wait()
     loads[1].wait()
 
-    def run(hop, shift):
-        anchor = position - shift
-        slot = shift + hops
-
-        @pl.when(inside(anchor))
-        def _():
-            sign = shift if hop is None else jnp.where(shift > 0, 1, -1)
-
-            @pl.when(shift != 0)
-            def _():
-                query_copy(slot, anchor).wait_recv()
-
+    for hop in order:
+        pair = (hop, -hop)
+        for d in pair:
+
+            @pl.when(inside(position - d))
+            def _(d=d):
+                query_copy(d + hops, position - d).wait_recv()
+
+        @pl.when(inside(position - hop) | inside(position + hop))
+        def _(hop=hop, pair=pair):
             attend(
-                hop, sign, pack_ref.at[slot], k_ref, v_ref, slope_ref, score_ref,
-                out_ref.at[slot], stat_ref.at[slot],
-            )
-
-            @pl.when(shift != 0)
-            def _():
-                stat_copy(slot, anchor).start()
-                out_copy(slot, anchor).start()
-
-    def near(i, _):
-        run(None, i - 3 * (i // 2))
-        return 0
-
-    lax.fori_loop(0, 3, near, 0)
-    for hop in order[1:]:
-
-        def far(i, _, hop=hop):
-            run(hop, (2 * i - 1) * hop)
-            return 0
-
-        lax.fori_loop(0, 2, far, 0)
+                hop, (1, -1), [d + hops for d in pair], pack_ref, k_ref, v_ref, slope_ref,
+                score_ref, out_ref, stat_ref,
+            )
+
+        for d in pair:
+
+            @pl.when(inside(position - d))
+            def _(d=d):
+                stat_copy(d + hops, position - d).start()
+                out_copy(d + hops, position - d).start()
+
+    attend(
+        0, (1,), [hops], pack_ref, k_ref, v_ref, slope_ref, score_ref, out_ref, stat_ref
+    )
 
     back_stat_ref[hops] = stat_ref[hops]
     for d in offsets:
@@ -339,7 +349,7 @@
             pltpu.VMEM((slots, 2 * groups, rows), jnp.float32),
             pltpu.VMEM((slots, rows, width), jnp.bfloat16),
             pltpu.VMEM((slots, 2 * groups, rows), jnp.float32),
-            pltpu.VMEM((2, rows, bins), jnp.float32),
+            pltpu.VMEM((2, 2 * rows, bins), jnp.float32),
             pltpu.VMEM((rows, width), jnp.float32),
             pltpu.VMEM((head_count - 1, rows, piece), jnp.bfloat16),
             pltpu.VMEM((head_count - 1, rows, piece), jnp.bfloat16),

time: 45 us -> 43.2 us (0.960)
  the two profiles are of different devices: /device:TPU:3 before, /device:TPU:13 now
where the time goes in v3:
time: 43.2 us; the launch traced here: 43.1 us
  Pallas kernels  41.5 us (96%)
  other arithmetic  1.58 us (4%)
    pallas_call x1, Pallas kernels, local(): pl.pallas_call(functools.partial(attend_kernel, hops, seq_count, head_cou...  41.5 us
    convert_element_type x1, other arithmetic, local(): return result.astype(jnp.bfloat16)  1.58 us

profile of v3, /device:TPU:13, one launch (start us, length us, event | category | flops | bytes accessed | tf_op | source)
XLA Modules:
  0.0 43.1 jit_solution(6997115742491540812)
XLA Ops:
  0.0 41.5 %shard_map.91 = f32[128,384]{1,0:T(8,128)} custom-call(bf16[128,384]{1,0:T(8,128)(2,1)} %query_ref.1, s32[1,128]{1,0:T(1,128)} %bitcast.3, s32[1,128]{1,0:T(1,128)} %bitcast.4, s32[1,128]{1,0:T(1,128)} %bitcast.5, bf16[128,384]{1,0:T(8,128)(2,1)} %embed_ref.1, bf16[2048,384]{1,0:T(8,128)(2,1)} %k_hbm.1, bf16[2048,384]{1,0:T(8,128)(2,1)} %v_hbm.1, ...), custom_call_target="tpu_custom_call" | custom-call | tf_op jit(solution)/shard_map/pallas_call | solution.py:338
  41.5 1.6 %convert_element_type.3 = bf16[128,384]{1,0:T(8,128)(2,1)} convert(f32[128,384]{1,0:T(8,128)} %shard_map.91) | non-fusion elementwise | flops 49152 | bytes 294912 | tf_op jit(solution)/shard_map/convert_element_type | solution.py:372

commit v4 on v3

--- a/solution.py
+++ b/solution.py
@@ -187,11 +187,57 @@
     around = jnp.minimum(position, hops) + jnp.minimum(seq_count - 1 - position, hops)
     pl.semaphore_wait(barrier, around + head_count - 1)
 
-    def query_copy(slot, target):
+    side = 1 - 2 * lax.rem(position, 2)
+    partner = position + side
+
+    def query_copy(source, slot, target, send):
         return pltpu.make_async_remote_copy(
-            src_ref=pack_ref.at[hops], dst_ref=pack_ref.at[slot], send_sem=q_send.at[slot],
+            src_ref=pack_ref.at[source], dst_ref=pack_ref.at[slot], send_sem=q_send.at[send],
             recv_sem=q_recv.at[slot], device_id=(target, mine), device_id_type=MESH,
         )
+
+    sends = [
+        (True, lambda: query_copy(hops, hops + side, partner, 0)),
+        (inside(position + 2), lambda: query_copy(hops, hops + 2, position + 2, 1)),
+        (inside(position - 2), lambda: query_copy(hops, hops - 2, position - 2, 2)),
+    ]
+    onward, final = [], []
+    for s, send in ((1, 3), (-1, 5)):
+        onward += [
+            (
+                inside(position - 2 * s) & inside(position + 2 * s),
+                lambda s=s, send=send: query_copy(
+                    hops + 2 * s, hops + 4 * s, position + 2 * s, send
+                ),
+            ),
+            (
+                inside(position - 2 * s),
+                lambda s=s, send=send: query_copy(
+                    hops + 2 * s, hops + 2 * s + side, partner, send + 1
+                ),
+            ),
+        ]
+        final.append(
+            (
+                inside(position - 4 * s) & (side == -s),
+                lambda s=s: query_copy(hops + 4 * s, hops + 3 * s, partner, 7),
+            )
+        )
+
+    def each(entries, act):
+        for condition, make in entries:
+            if condition is True:
+                act(make())
+            else:
+
+                @pl.when(condition)
+                def _(make=make):
+                    act(make())
+
+    def arrived(d):
+        @pl.when(inside(position - d))
+        def _():
+            query_copy(hops, d + hops, partner, 0).wait_recv()
 
     def out_copy(slot, target):
         return pltpu.make_async_remote_copy(
@@ -205,13 +251,7 @@
             recv_sem=s_recv.at[slot], device_id=(target, mine), device_id_type=MESH,
         )
 
-    order = [1] + list(range(hops, 1, -1))
-    for hop in order:
-        for d in (hop, -hop):
-
-            @pl.when(inside(position + d))
-            def _(d=d):
-                query_copy(d + hops, position + d).start()
+    each(sends, lambda copy: copy.start())
 
     for d in offsets:
 
@@ -222,13 +262,18 @@
     loads[0].wait()
     loads[1].wait()
 
-    for hop in order:
+    arrived(2)
+    arrived(-2)
+    each(onward, lambda copy: copy.start())
+    for hop in (2, 1, 4, 3):
         pair = (hop, -hop)
-        for d in pair:
-
-            @pl.when(inside(position - d))
-            def _(d=d):
-                query_copy(d + hops, position - d).wait_recv()
+        if hop == 1:
+            arrived(4)
+            arrived(-4)
+            each(final, lambda copy: copy.start())
+        if hop in (1, 3):
+            for d in pair:
+                arrived(d)
 
         @pl.when(inside(position - hop) | inside(position + hop))
         def _(hop=hop, pair=pair):
@@ -310,13 +355,10 @@
         result = result + head_ref[r - 1].astype(jnp.float32)
     result_ref[...] = result
 
+    each(sends + onward + final, lambda copy: copy.wait_send())
     for r in range(1, head_count):
         head_copy(r, lax.rem(mine + r, head_count)).wait_send()
     for d in offsets:
-
-        @pl.when(inside(position + d))
-        def _(d=d):
-            query_copy(d + hops, position + d).wait_send()
 
         @pl.when(inside(position - d))
         def _(d=d):

time: 43.2 us -> 40.1 us (0.928)
  the two profiles are of different devices: /device:TPU:13 before, /device:TPU:1 now
where the time goes in v4:
time: 40.1 us; the launch traced here: 40 us
  Pallas kernels  38.4 us (96%)
  other arithmetic  1.58 us (4%)
    pallas_call x1, Pallas kernels, local(): pl.pallas_call(functools.partial(attend_kernel, hops, seq_count, head_cou...  38.4 us
    convert_element_type x1, other arithmetic, local(): return result.astype(jnp.bfloat16)  1.58 us

profile of v4, /device:TPU:1, one launch (start us, length us, event | category | flops | bytes accessed | tf_op | source)
XLA Modules:
  0.0 40.0 jit_solution(9545918947443018157)
XLA Ops:
  0.0 38.4 %shard_map.91 = f32[128,384]{1,0:T(8,128)} custom-call(bf16[128,384]{1,0:T(8,128)(2,1)} %query_ref.1, s32[1,128]{1,0:T(1,128)} %bitcast.3, s32[1,128]{1,0:T(1,128)} %bitcast.4, s32[1,128]{1,0:T(1,128)} %bitcast.5, bf16[128,384]{1,0:T(8,128)(2,1)} %embed_ref.1, bf16[2048,384]{1,0:T(8,128)(2,1)} %k_hbm.1, bf16[2048,384]{1,0:T(8,128)(2,1)} %v_hbm.1, ...), custom_call_target="tpu_custom_call" | custom-call | tf_op jit(solution)/shard_map/pallas_call | solution.py:380
  38.4 1.6 %convert_element_type.3 = bf16[128,384]{1,0:T(8,128)(2,1)} convert(f32[128,384]{1,0:T(8,128)} %shard_map.91) | non-fusion elementwise | flops 49152 | bytes 294912 | tf_op jit(solution)/shard_map/convert_element_type | solution.py:414
